TPU v7x, 128 devices: a whole 4x4x4 slice. The times are simulated.
128 devices in a mesh: dom: 128 (over x, y, z, core).
Axes of the slice: x: 4, y: 4, z: 4, core: 2. Of those that a mesh axis runs over, the one named last changes fastest.
Arguments:
- features: bfloat16 [524288, 128], P('dom'), may hold values from -6 to 6
- hubs: bfloat16 [8192, 128], P('dom'), may hold values from -6 to 6
- weight: bfloat16 [128, 128], replicated, may hold values from -0.5 to 0.5
- bias: float32 [128], replicated, may hold values from -3 to 3
- cotangent: bfloat16 [524288, 128], P('dom'), may hold values from -6 to 6
- tiles: bfloat16 [65536, 128, 128], P('dom'), may hold values from 0 to 0.049804688
- tile_blocks: int32 [65536, 2], P('dom'), may hold values from 0 to 95, as said below
- tile_count: int32 [128], P('dom'), may hold values from 96 to 512, as said below
- halo_send: int32 [128, 128, 32], P('dom'), may hold values from 0 to 4095
- replica_rows: int32 [128, 128, 32], P('dom'), may hold values from 0 to 63
Outputs:
- activations: bfloat16 [524288, 128], P('dom')
- saliency: float32 [524288, 128], P('dom')
- hub_saliency: float32 [8192, 128], P('dom')
Inputs may be any that keep to these rules, and one draw needn't show every extreme that they name: `tile_blocks`: the first 96 tile slots of each partition name every column block of its extended table once; the others name any row and column blocks. `tile_count`: some partition has all 512 slots live.
All inputs are finite; a program needn't handle non-finite values.
Results may differ from a plain program's by a relative error of at most 0.0054.
Values may be sent and summed in bfloat16 or wider, within the bound.
No kernel may reach another device: no remote copies, remote signals or barrier semaphores. Data moves between devices by JAX's collectives and lax.ppermute only.
A program may use at most 128 MiB of HBM per device.

v0:
```python
import functools

import jax
import jax.numpy as jnp
from jax import lax
from jax.experimental import pallas as pl
from jax.experimental.pallas import tpu as pltpu
from jax.sharding import PartitionSpec as P


VMEM = pltpu.VMEM
SMEM = pltpu.SMEM
F32 = jnp.float32
BF16 = jnp.bfloat16
I32 = jnp.int32
PAIRS = 8
CHAINS = 6
NT = (((1,), (1,)), ((), ()))


def whole(space):
    return pl.BlockSpec(memory_space=space)


def params(mib):
    return pltpu.CompilerParams(vmem_limit_bytes=mib << 20)


def in_hbm(array):
    return pltpu.with_memory_space_constraint(array, pltpu.HBM)


def outgoing_kernel(send_ref, feat_ref, hub_ref, wanted_ref, out_ref, wide, stage, names):
    step = pl.program_id(0)
    chunk = out_ref.shape[0]
    rows = send_ref.shape[0]
    width = feat_ref.shape[1]
    half = hub_ref.shape[0] // 2

    @pl.when(step == 0)
    def _():
        wide[...] = feat_ref[...].astype(F32)
        tall = jnp.concatenate([wanted_ref[...].astype(F32)] * (width // rows), axis=0)
        names[...] = jnp.transpose(tall)

    halves = (hub_ref[:half, :], hub_ref[half:, :])

    @pl.loop(0, chunk // 2)
    def _(pair):
        for side in range(2):
            q = pair * 2 + side
            for j in range(rows):
                row = send_ref[j, step * chunk + q]
                stage[side, pl.ds(j, 1), :] = wide[pl.ds(row, 1), :]
        for side in range(2):
            q = pair * 2 + side
            out_ref[q, 0:rows, :] = stage[side].astype(BF16)
            out_ref[q, rows : rows + half, :] = halves[side]
            line = names[pl.ds(step * chunk + q, 1), :]
            out_ref[q, rows + half :, :] = jnp.broadcast_to(line, (8, width)).astype(BF16)


def outgoing_rows(send, features, hubs, wanted):
    rows, parties = send.shape
    width = features.shape[1]
    total = rows + hubs.shape[0] // 2 + 8
    steps = 4
    chunk = parties // steps
    return pl.pallas_call(
        outgoing_kernel,
        name="outgoing_rows",
        grid=(steps,),
        in_specs=[
            whole(SMEM),
            pl.BlockSpec(features.shape, lambda i: (0, 0)),
            pl.BlockSpec(hubs.shape, lambda i: (0, 0)),
            pl.BlockSpec(wanted.shape, lambda i: (0, 0)),
        ],
        out_specs=pl.BlockSpec((chunk, total, width), lambda i: (i, 0, 0)),
        out_shape=jax.ShapeDtypeStruct((parties, total, width), BF16),
        scratch_shapes=[
            VMEM(features.shape, F32),
            VMEM((2, rows, width), F32),
            VMEM((parties, width), F32),
        ],
        compiler_params=params(60),
        cost_estimate=pl.CostEstimate(flops=0, bytes_accessed=30 << 20, transcendentals=0),
    )(send, features, hubs, wanted)


def plan_kernel(blocks, count_ref, side_ref, places_ref, wanted_ref, list_ref, group_ref, hot_ref):
    slots = places_ref.shape[1]
    length = list_ref.shape[1]
    lanes = 128
    count = count_ref[0]
    row = places_ref[0:1, :]
    column = places_ref[1:2, :]
    slot = lax.broadcasted_iota(I32, (1, slots), 1)
    kind = jnp.where(column < blocks, 0, jnp.where(column < 2 * blocks, 1, 2))
    key = jnp.where(slot < count, kind * blocks + row, lanes - 1).astype(F32)
    entry = (slot | (row << 10) | (column << 16)).astype(F32)
    lines = jnp.concatenate([key, entry] + [jnp.zeros_like(key)] * 6, axis=0)
    tall = jnp.transpose(lines)
    key_tall, entry_tall = tall[:, 0:1], tall[:, 1:2]
    lane = lax.broadcasted_iota(I32, (1, lanes), 1)
    member = key_tall == lane.astype(F32)
    counts = jnp.sum(jnp.where(member, 1.0, 0.0), axis=0, keepdims=True)
    halves = jnp.where(lane < 3 * blocks, (counts.astype(I32) + 1) // 2, 0)
    before = jnp.where(
        lax.broadcasted_iota(I32, (lanes, lanes), 0) < lax.broadcasted_iota(I32, (lanes, lanes), 1), 1.0, 0.0
    ).astype(BF16)
    prefix = jnp.dot(
        jnp.broadcast_to(halves.astype(F32), (16, lanes)).astype(BF16), before, preferred_element_type=F32
    )[0:1, :].astype(I32)
    bucket = lane // blocks
    offset = prefix
    groups = jnp.zeros_like(lane)
    begun = jnp.zeros((1, 1), I32)
    passed = jnp.zeros((1, 1), I32)
    for k in range(3):
        pairs = jnp.sum(jnp.where(bucket == k, halves, 0), axis=1, keepdims=True)
        turns = (pairs + PAIRS - 1) // PAIRS
        offset = jnp.where(bucket == k, prefix + (begun * PAIRS - passed), offset)
        groups = jnp.where(lane == k, begun, groups)
        groups = jnp.where(lane == 3 + k, turns, groups)
        begun = begun + turns
        passed = passed + pairs
    group_ref[...] = groups
    first = jnp.sum(jnp.where(member, offset.astype(F32), 0.0), axis=1, keepdims=True)
    earlier = lax.broadcasted_iota(I32, (slots, slots), 1) < lax.broadcasted_iota(I32, (slots, slots), 0)
    index = jnp.sum(jnp.where((key_tall == key) & earlier, 1.0, 0.0), axis=1, keepdims=True)
    place = jnp.where(key_tall < 3 * blocks, 2.0 * first + index, -1.0)
    spare = float((blocks << 10) | (3 * blocks << 16))
    target = lax.broadcasted_iota(I32, (1, length), 1).astype(F32)
    placed = jnp.sum(jnp.where(place == target, entry_tall - spare, 0.0), axis=0, keepdims=True)
    list_ref[...] = (placed + spare).astype(I32)

    rows, parties = wanted_ref.shape
    group = hot_ref.shape[1] // rows
    half = hot_ref.shape[2] // 2 // group
    wanted = wanted_ref[...]
    member_of = lax.broadcasted_iota(I32, (rows, parties), 1) % group
    far = ((wanted >= half).astype(I32) != side_ref[0]).astype(I32)
    spot = jnp.where(wanted >= half, wanted - half, wanted) + member_of * half + far * (group * half)
    lane = lax.broadcasted_iota(I32, (rows, 2 * group * half), 1)
    for p in range(parties):
        hot = jnp.where(spot[:, p : p + 1] == lane, 1.0, 0.0)
        hot_ref[p // group, (p % group) * rows : (p % group + 1) * rows, :] = hot.astype(BF16)


def plan(count, side, places, wanted, blocks, tile):
    slots = places.shape[1]
    length = list_length(slots, blocks)
    return pl.pallas_call(
        functools.partial(plan_kernel, blocks),
        name="plan",
        in_specs=[whole(SMEM), whole(SMEM), whole(VMEM), whole(VMEM)],
        out_specs=[whole(VMEM)] * 3,
        out_shape=[
            jax.ShapeDtypeStruct((1, length), I32),
            jax.ShapeDtypeStruct((1, 128), I32),
            jax.ShapeDtypeStruct((blocks, tile, 2 * tile), BF16),
        ],
        compiler_params=params(60),
        cost_estimate=pl.CostEstimate(flops=10**7, bytes_accessed=8 << 20, transcendentals=0),
    )(count, side, places, wanted)


def unpack(entry):
    return entry & 1023, (entry >> 10) & 63, entry >> 16


def fetch_tiles(list_ref, begin, first, last, tiles_ref, store, sems):
    @pl.loop(first, last)
    def _(turn):
        for u in range(2 * PAIRS):
            tile, _, _ = unpack(list_ref[0, (begin + turn) * 2 * PAIRS + u])
            pltpu.make_async_copy(tiles_ref.at[tile], store.at[turn, u], sems.at[turn]).start()


def tile_loop(list_ref, begin, first, last, tiles_ref, store, sems, body):
    @pl.loop(first, last)
    def _(turn):
        if sems is not None:
            pltpu.make_async_copy(
                tiles_ref.at[pl.ds(0, 2 * PAIRS)], store.at[turn], sems.at[turn]
            ).wait()
        for u in range(PAIRS):
            place = (begin + turn) * 2 * PAIRS + 2 * u
            _, row, left = unpack(list_ref[0, place])
            _, _, right = unpack(list_ref[0, place + 1])
            body(store[turn, 2 * u], store[turn, 2 * u + 1], row, left, right)


def list_length(slots, blocks):
    return -(-(slots + 3 * blocks + 6 * PAIRS) // 128) * 128


def store_scratch(tiles, blocks):
    groups = (tiles.shape[0] + 3 * blocks) // (2 * PAIRS) + 4
    return [
        VMEM((groups, 2 * PAIRS) + tiles.shape[1:], BF16),
        pltpu.SemaphoreType.DMA((groups,)),
    ]


def forward_body(total, table, base):
    spare = table.shape[0] - 1

    def body(first, second, row, left, right):
        values = jnp.concatenate([first, second], axis=1)
        left = jnp.minimum(left - base, spare)
        right = jnp.minimum(right - base, spare)
        rows = jnp.concatenate([table[left], table[right]], axis=0)
        total[row] += jnp.dot(values, rows, preferred_element_type=F32)

    return body


def backward_body(spread, swapped, base):
    spare = spread.shape[0] - 1

    def body(first, second, row, left, right):
        tile = first.shape[1]
        values = jnp.concatenate([first, second], axis=1)
        product = jnp.dot(swapped[row], values, preferred_element_type=F32)
        spread[jnp.minimum(left - base, spare)] += product[:, :tile]
        spread[jnp.minimum(right - base, spare)] += product[:, tile:]

    return body


def own_forward_kernel(list_ref, group_ref, feat_ref, tiles_ref, sum_ref, table, total, store, sems):
    blocks = feat_ref.shape[0]
    begin, turns = group_ref[0, 0], group_ref[0, 3]
    fetch_tiles(list_ref, begin, 0, turns, tiles_ref, store, sems)
    total[...] = jnp.zeros_like(total)
    table[:blocks] = feat_ref[...]
    table[blocks] = jnp.zeros(table.shape[1:], BF16)
    tile_loop(list_ref, begin, 0, turns, tiles_ref, store, sems, forward_body(total, table, 0))
    sum_ref[...] = total[:blocks]


def own_forward(lists, groups, features, tiles):
    tile = tiles.shape[1]
    blocks = features.shape[0] // tile
    width = features.shape[1]
    return pl.pallas_call(
        own_forward_kernel,
        name="own_forward",
        in_specs=[whole(SMEM), whole(SMEM), whole(VMEM), whole(pltpu.HBM)],
        out_specs=whole(VMEM),
        out_shape=jax.ShapeDtypeStruct((blocks, tile, width), F32),
        scratch_shapes=[VMEM((blocks + 1, tile, width), BF16), VMEM((blocks + 1, tile, width), F32)]
        + store_scratch(tiles, blocks),
        compiler_params=params(50),
        cost_estimate=pl.CostEstimate(flops=10**9, bytes_accessed=40 << 20, transcendentals=0),
    )(lists, groups, features.reshape(blocks, tile, width), in_hbm(tiles))


def boundary_forward_kernel(
    list_ref, group_ref, near_ref, start_ref, tiles_ref, sum_ref, table, total, store, sems, start_sem
):
    blocks, tile, width = sum_ref.shape
    group = near_ref.shape[0] // blocks
    begin, turns = group_ref[0, 1], group_ref[0, 4]
    start_copy = pltpu.make_async_copy(start_ref, total.at[pl.ds(0, blocks)], start_sem)
    start_copy.start()
    fetch_tiles(list_ref, begin, 0, turns, tiles_ref, store, sems)
    for b in range(blocks):
        table[b] = near_ref[b * group : (b + 1) * group, 0 : tile // group, :].reshape(tile, width)
    table[blocks] = jnp.zeros(table.shape[1:], BF16)
    start_copy.wait()
    tile_loop(list_ref, begin, 0, turns, tiles_ref, store, sems, forward_body(total, table, blocks))
    sum_ref[...] = total[:blocks]


def boundary_forward(lists, groups, arrived, start, tiles):
    blocks, tile, width = start.shape
    return pl.pallas_call(
        boundary_forward_kernel,
        name="boundary_forward",
        in_specs=[whole(SMEM)] * 2 + [whole(VMEM), whole(pltpu.HBM), whole(pltpu.HBM)],
        out_specs=whole(VMEM),
        out_shape=jax.ShapeDtypeStruct(start.shape, F32),
        scratch_shapes=[VMEM((blocks + 1, tile, width), BF16), VMEM((blocks + 1, tile, width), F32)]
        + store_scratch(tiles, blocks)
        + [pltpu.SemaphoreType.DMA],
        compiler_params=params(40),
        cost_estimate=pl.CostEstimate(flops=10**9, bytes_accessed=40 << 20, transcendentals=0),
    )(lists, groups, arrived, in_hbm(start), in_hbm(tiles))


def middle_kernel(
    list_ref, group_ref, near_ref, far_ref, hot_ref, start_ref, weight_ref, bias_ref, cot_ref, tiles_ref,
    act_out, back_out, grads_ref, act_ref, table, total, swapped, spread, parcel, store, sems, out_sems,
):
    blocks, tile, width = act_ref.shape
    group = near_ref.shape[0] // blocks
    rows = tile // group
    weight = weight_ref[...]
    near_turns, hub_turns = group_ref[0, 4], group_ref[0, 5]
    fetch_tiles(list_ref, group_ref[0, 2], 0, hub_turns, tiles_ref, store, sems)
    fetch_tiles(list_ref, group_ref[0, 1] - hub_turns, hub_turns, hub_turns + near_turns, tiles_ref, store, sems)
    total[:blocks] = start_ref[...]

    @pl.loop(0, blocks // 4)
    def _(turn):
        for i in range(4):
            b = turn * 4 + i
            near = near_ref[pl.ds(b * group, group), rows : 2 * rows, :].reshape(tile, width)
            far = far_ref[pl.ds(b * group, group), rows : 2 * rows, :].reshape(tile, width)
            picked = jnp.dot(hot_ref[b], jnp.concatenate([near, far], axis=0), preferred_element_type=F32)
            table[b] = picked.astype(BF16)

    table[blocks] = jnp.zeros(table.shape[1:], BF16)
    tile_loop(
        list_ref, group_ref[0, 2], 0, hub_turns, tiles_ref, store, sems, forward_body(total, table, 2 * blocks)
    )

    @pl.loop(0, blocks // 4)
    def _(turn):
        for i in range(4):
            b = turn * 4 + i
            preact = jnp.dot(total[b].astype(BF16), weight, preferred_element_type=F32) + bias_ref[...]
            sigmoid = 0.5 * jnp.tanh(0.5 * preact) + 0.5
            act_ref[b] = (preact * sigmoid).astype(BF16)
            slope = sigmoid * (1.0 + preact * (1.0 - sigmoid))
            upstream = (cot_ref[b].astype(F32) * slope).astype(BF16)
            swapped[b] = lax.dot_general(weight, upstream, NT, preferred_element_type=F32).astype(BF16)

    results = (
        pltpu.make_async_copy(act_ref, act_out, out_sems.at[blocks // 2]),
        pltpu.make_async_copy(swapped.at[pl.ds(0, blocks)], back_out, out_sems.at[blocks // 2 + 1]),
    )
    for result in results:
        result.start()
    spread[...] = jnp.zeros_like(spread)
    add = backward_body(spread, swapped, blocks)
    tile_loop(list_ref, group_ref[0, 2], 0, hub_turns, tiles_ref, store, None, add)
    tile_loop(
        list_ref, group_ref[0, 1] - hub_turns, hub_turns, hub_turns + near_turns, tiles_ref, store, sems, add
    )

    chunk = 2 * group

    def send(turn):
        return pltpu.make_async_copy(
            parcel.at[pl.ds(turn * chunk, chunk)], grads_ref.at[pl.ds(turn * chunk, chunk)], out_sems.at[turn]
        )

    @pl.loop(0, blocks // 2)
    def _(turn):
        for i in range(2):
            b = turn * 2 + i
            for part in range(2):
                out = jnp.transpose(spread[part * blocks + b].astype(BF16))
                parcel[pl.ds(b * group, group), part * rows : (part + 1) * rows, :] = out.reshape(
                    group, rows, width
                )
        send(turn).start()

    @pl.loop(0, blocks // 2)
    def _(turn):
        send(turn).wait()

    for result in results:
        result.wait()


def middle(lists, groups, arrived, other, hot, start, weight, bias, cotangent, tiles):
    blocks, tile, width = start.shape
    parties = arrived.shape[0]
    rows = blocks * tile // parties
    return pl.pallas_call(
        middle_kernel,
        name="middle",
        in_specs=[whole(SMEM)] * 2
        + [whole(VMEM)] * 7
        + [whole(pltpu.HBM)],
        out_specs=[whole(pltpu.HBM)] * 3,
        out_shape=[
            pltpu.HBM((blocks, tile, width), BF16),
            pltpu.HBM((blocks, width, tile), BF16),
            pltpu.HBM((parties, 2 * rows, width), BF16),
        ],
        scratch_shapes=[
            VMEM((blocks, tile, width), BF16),
            VMEM((blocks + 1, tile, width), BF16),
            VMEM((blocks + 1, tile, width), F32),
            VMEM((blocks + 1, width, tile), BF16),
            VMEM((2 * blocks + 1, width, tile), F32),
            VMEM((parties, 2 * rows, width), BF16),
        ]
        + store_scratch(tiles, blocks)
        + [pltpu.SemaphoreType.DMA((blocks // 2 + 2,))],
        compiler_params=params(42),
        cost_estimate=pl.CostEstimate(flops=4 * 10**9, bytes_accessed=60 << 20, transcendentals=10**6),
    )(
        lists, groups, arrived, other, hot, start, weight, bias, cotangent.reshape(blocks, tile, width), in_hbm(tiles)
    )


def own_backward_kernel(
    list_ref, group_ref, back_ref, names_ref, tiles_ref, own_ref, hot_ref, swapped, spread, store, sems, back_sem
):
    blocks = back_ref.shape[0]
    begin, turns = group_ref[0, 0], group_ref[0, 3]
    back_copy = pltpu.make_async_copy(back_ref, swapped.at[pl.ds(0, blocks)], back_sem)
    back_copy.start()
    fetch_tiles(list_ref, begin, 0, turns, tiles_ref, store, sems)
    spread[...] = jnp.zeros_like(spread)
    back_copy.wait()
    tile_loop(list_ref, begin, 0, turns, tiles_ref, store, sems, backward_body(spread, swapped, 0))

    @pl.loop(0, blocks // 2)
    def _(turn):
        for i in range(2):
            own_ref[turn * 2 + i] = jnp.transpose(spread[turn * 2 + i])

    parties, total, width = names_ref.shape
    group = parties // blocks
    rows = width // group
    names = names_ref[:, total - 8, :].astype(F32)
    party = lax.broadcasted_iota(I32, names.shape, 0)
    lane = lax.broadcasted_iota(I32, names.shape, 1)
    names = jnp.where(lane // rows == party % group, names, 0.0).astype(BF16)
    block = lax.broadcasted_iota(I32, (blocks, parties), 0)
    gather = jnp.where(lax.broadcasted_iota(I32, (blocks, parties), 1) // group == block, 1.0, 0.0)
    lines = jnp.dot(gather.astype(BF16), names, preferred_element_type=F32)
    hub = lax.broadcasted_iota(I32, hot_ref.shape[1:], 0).astype(F32)
    for b in range(blocks):
        hot_ref[b] = jnp.where(hub == lines[b : b + 1, :], 1.0, 0.0).astype(BF16)


def own_backward(lists, groups, back, arrived, tiles, hubs):
    blocks, width, tile = back.shape
    return pl.pallas_call(
        own_backward_kernel,
        name="own_backward",
        in_specs=[whole(SMEM)] * 2 + [whole(pltpu.HBM), whole(VMEM), whole(pltpu.HBM)],
        out_specs=[whole(VMEM)] * 2,
        out_shape=[
            jax.ShapeDtypeStruct((blocks, tile, width), F32),
            jax.ShapeDtypeStruct((blocks, hubs, width), BF16),
        ],
        scratch_shapes=[VMEM((blocks + 1, width, tile), BF16), VMEM((blocks + 1, width, tile), F32)]
        + store_scratch(tiles, blocks)
        + [pltpu.SemaphoreType.DMA],
        compiler_params=params(50),
        cost_estimate=pl.CostEstimate(flops=10**9, bytes_accessed=40 << 20, transcendentals=0),
    )(lists, groups, in_hbm(back), arrived, in_hbm(tiles))


def returned_kernel(send_ref, own_ref, back_ref, hot_ref, sal_ref, hub_ref, stage, hot, chains, sems):
    rows, parties = send_ref.shape
    blocks, _, width = hot_ref.shape
    group = parties // blocks
    own_copy = pltpu.make_async_copy(own_ref, sal_ref, sems.at[0])
    hot_copy = pltpu.make_async_copy(hot_ref, hot, sems.at[1])
    own_copy.start()
    hot_copy.start()
    for chain in chains:
        chain[...] = jnp.zeros_like(chain)
    own_copy.wait()
    sums = (sal_ref,) + tuple(chains)

    @pl.loop(0, parties)
    def _(q):
        stage[...] = back_ref[q, 0:rows, :].astype(F32)
        for j in range(rows):
            chain = sums[j % len(sums)]
            row = send_ref[j, q]
            chain[pl.ds(row, 1), :] += stage[pl.ds(j, 1), :]

    total = sal_ref[...]
    for chain in chains:
        total = total + chain[...]
    sal_ref[...] = total

    hot_copy.wait()
    total = jnp.zeros(hub_ref.shape, F32)
    for b in range(0, blocks, 2):
        grads = back_ref[b * group : (b + 2) * group, rows:, :].reshape(2 * group * rows, width)
        pair = jnp.concatenate([hot[b], hot[b + 1]], axis=1)
        total += jnp.dot(pair, grads, preferred_element_type=F32)
    hub_ref[...] = total


def returned_rows(send, own, returned, hot):
    rows, _ = send.shape
    own_rows, width = own.shape
    return pl.pallas_call(
        returned_kernel,
        name="returned_rows",
        in_specs=[whole(SMEM), whole(pltpu.HBM), whole(VMEM), whole(pltpu.HBM)],
        out_specs=[whole(VMEM)] * 2,
        out_shape=[
            jax.ShapeDtypeStruct((own_rows, width), F32),
            jax.ShapeDtypeStruct((hot.shape[1], width), F32),
        ],
        scratch_shapes=[
            VMEM((rows, width), F32),
            VMEM(hot.shape, BF16),
            [VMEM((own_rows, width), F32)] * (CHAINS - 1),
            pltpu.SemaphoreType.DMA((2,)),
        ],
        compiler_params=params(32),
        cost_estimate=pl.CostEstimate(flops=10**8, bytes_accessed=40 << 20, transcendentals=0),
    )(send, in_hbm(own), returned, in_hbm(hot))


def body(
    features, hubs, weight, bias, cotangent, tiles, tile_blocks, tile_count, halo_send, replica_rows
):
    own_rows, width = features.shape
    tile = tiles.shape[1]
    blocks = own_rows // tile
    send = halo_send[0].T
    wanted = replica_rows[0].T
    parties = send.shape[1]
    side = (lax.axis_index("dom") % 2).astype(I32).reshape(1)

    pairs = [(i, i ^ 1) for i in range(parties)]

    outgoing = outgoing_rows(send, features, hubs, wanted)
    arrived = lax.all_to_all(outgoing, "dom", split_axis=0, concat_axis=0, tiled=True)
    lists, groups, hot = plan(tile_count, side, tile_blocks.T, wanted, blocks, tile)
    start = own_forward(lists, groups, features, tiles)
    other = lax.ppermute(arrived, "dom", pairs)
    start = boundary_forward(lists, groups, arrived, start, tiles)
    act, back, grads = middle(lists, groups, arrived, other, hot, start, weight, bias.reshape(1, -1), cotangent, tiles)
    returned = lax.all_to_all(grads, "dom", split_axis=0, concat_axis=0, tiled=True)
    own, hub_hot = own_backward(lists, groups, back, arrived, tiles, hubs.shape[0])
    saliency, hub_saliency = returned_rows(send, own.reshape(own_rows, width), returned, hub_hot)
    return act.reshape(own_rows, width), saliency, hub_saliency


def solution(mesh):
    placed = (
        P("dom", None),
        P("dom", None),
        P(),
        P(),
        P("dom", None),
        P("dom", None, None),
        P("dom", None),
        P("dom"),
        P("dom", None, None),
        P("dom", None, None),
    )
    return jax.shard_map(
        body,
        mesh=mesh,
        in_specs=placed,
        out_specs=(P("dom", None), P("dom", None), P("dom", None)),
        check_vma=False,
    )
```

profile of v0, /device:TPU:0, one launch (start us, length us, event | category | flops | bytes accessed | tf_op | source)
XLA Modules:
  0.0 139.2 jit_solution(228389535981107825)
XLA Ops:
  0.6 7.6 %outgoing_rows.1 = bf16[128,72,128]{2,1,0:T(8,128)(2,1)} custom-call(s32[32,128]{1,0:T(8,128)} %bitcast.16, bf16[4096,128]{1,0:T(8,128)(2,1)} %feat_ref.1, bf16[64,128]{1,0:T(8,128)(2,1)} %hub_ref.1, s32[32,128]{1,0:T(8,128)} %bitcast.19), custom_call_target="tpu_custom_call" | custom-call | bytes 31457280 | tf_op jit(solution)/shard_map/outgoing_rows/pallas_call | solution.py:69
  8.2 0.0 copy-start.2
  8.2 44.6 %all_to_all.10.near_ref.names_ref = bf16[128,72,128]{2,1,0:T(8,128)(2,1)S(1)} all-to-all(bf16[128,72,128]{2,1,0:T(8,128)(2,1)} %outgoing_rows.1), channel_id=1, replica_groups=mesh['dom'=128] {'dom'}, dimensions={0} | all-to-all | bytes 4718592 | tf_op jit(solution)/shard_map/all_to_all | solution.py:527
  52.8 0.0 collective-permute-start
  53.5 3.6 %plan.1 = (s32[1,768]{1,0:T(1,128)}, s32[1,128]{1,0:T(1,128)}, bf16[32,128,256]{2,1,0:T(8,128)(2,1)}) custom-call(s32[1]{0:T(128)S(6)} %copy.13.count_ref, s32[1]{0:T(128)} %bitcast.side_ref, s32[2,512]{1,0:T(2,128)} %bitcast.22, s32[32,128]{1,0:T(8,128)} %bitcast.20), custom_call_target="tpu_custom_call" | custom-call | flops 10000000 | bytes 8388608 | tf_op jit(solution)/shard_map/plan/pallas_call | solution.py:154
  57.1 0.0 copy-done.2
  57.1 0.7 copy-done.8
  57.8 0.7 copy-done.11
  58.4 4.1 %own_forward.1.start_ref = f32[32,128,128]{2,1,0:T(8,128)S(1)} custom-call(s32[1,768]{1,0:T(1,128)S(1)} %copy-done.8, s32[1,128]{1,0:T(1,128)S(1)} %copy-done.11, bf16[32,128,128]{2,1,0:T(8,128)(2,1)S(1)} %bitcast.13, bf16[512,128,128]{2,1,0:T(8,128)(2,1)} %tiles_ref.7), custom_call_target="tpu_custom_call" | custom-call | flops 1000000000 | bytes 41943040 | tf_op jit(solution)/shard_map/own_forward/pallas_call | solution.py:248
  62.5 0.0 copy-start.1
  62.5 1.4 copy-done.1
  63.9 0.0 copy-start.12
  63.9 0.0 copy-start.13
  63.9 4.8 %boundary_forward.1.start_ref = f32[32,128,128]{2,1,0:T(8,128)S(1)} custom-call(s32[1,768]{1,0:T(1,128)S(1)} %copy-done.8, s32[1,128]{1,0:T(1,128)S(1)} %copy-done.11, bf16[128,72,128]{2,1,0:T(8,128)(2,1)S(1)} %all_to_all.10.near_ref.names_ref, f32[32,128,128]{2,1,0:T(8,128)} %copy-done.1, bf16[512,128,128]{2,1,0:T(8,128)(2,1)} %tiles_ref.7), custom_call_target="tpu_custom_call" | custom-call | flops 1000000000 | bytes 41943040 | tf_op jit(solution)/shard_map/boundary_forward/pallas_call | solution.py:280
  68.8 0.0 collective-permute-done.far_ref
  68.8 0.0 copy-done
  68.8 0.0 copy-done.4
  68.8 0.0 copy-done.5
  68.8 0.0 copy-done.9
  68.8 0.0 copy-done.10
  68.8 0.0 copy-done.12
  68.8 0.0 copy-done.13
  68.8 17.6 %middle.1 = (bf16[32,128,128]{2,1,0:T(8,128)(2,1)}, bf16[32,128,128]{2,1,0:T(8,128)(2,1)}, bf16[128,64,128]{2,1,0:T(8,128)(2,1)}) custom-call(s32[1,768]{1,0:T(1,128)S(1)} %copy-done.9, s32[1,128]{1,0:T(1,128)S(1)} %copy-done.12, bf16[128,72,128]{2,1,0:T(8,128)(2,1)S(1)} %all_to_all.10.near_ref.names_ref, ...), custom_call_target="tpu_custom_call" | custom-call | flops 4000000000 | bytes 62914560 | tf_op jit(solution)/shard_map/middle/pallas_call | solution.py:375
  86.5 12.7 %all-to-all-start.1 = ((bf16[128,64,128]{2,1,0:T(8,128)(2,1)}), bf16[128,64,128]{2,1,0:T(8,128)(2,1)S(1)}, u32[]{:S(2)}, u32[]{:S(2)}) async-start(bf16[128,64,128]{2,1,0:T(8,128)(2,1)} %get-tuple-element.19), calls=%async_computation.1 | async-start | bytes 4194304 | tf_op jit(solution)/shard_map/all_to_all | solution.py:533
  99.2 0.0 copy-start.7
  99.2 7.4 %own_backward.1 = (f32[32,128,128]{2,1,0:T(8,128)S(1)}, bf16[32,64,128]{2,1,0:T(8,128)(2,1)S(1)}) custom-call(s32[1,768]{1,0:T(1,128)S(1)} %copy-done.9, s32[1,128]{1,0:T(1,128)S(1)} %copy-done.12, bf16[32,128,128]{2,1,0:T(8,128)(2,1)} %get-tuple-element.17.back_ref, bf16[128,72,128]{2,1,0:T(8,128)(2,1)} %copy-done, bf16[512,128,128]{2,1,0:T(8,128)(2,1)} %tiles_ref.7), custom_call_target="tpu_custom_call" | custom-call | flops 1000000000 | bytes 41943040 | tf_op jit(solution)/shard_map/own_backward/pallas_call | solution.py:438
  106.7 0.0 copy-start.3
  106.7 1.3 copy-done.3
  108.0 0.8 copy-done.6
  108.8 21.0 %all-to-all-done.1.back_ref = bf16[128,64,128]{2,1,0:T(8,128)(2,1)S(1)} async-done(((bf16[128,64,128]{2,1,0:T(8,128)(2,1)}), bf16[128,64,128]{2,1,0:T(8,128)(2,1)S(1)}, u32[]{:S(2)}, u32[]{:S(2)}) %all-to-all-start.1) | async-done | bytes 2097184 | tf_op jit(solution)/shard_map/all_to_all | solution.py:533
  129.8 0.0 copy-done.7
  129.8 9.4 %returned_rows.1 = (f32[4096,128]{1,0:T(8,128)}, f32[64,128]{1,0:T(8,128)}) custom-call(s32[32,128]{1,0:T(8,128)S(1)} %bitcast.17, f32[4096,128]{1,0:T(8,128)} %bitcast.14, bf16[128,64,128]{2,1,0:T(8,128)(2,1)S(1)} %all-to-all-done.1.back_ref, bf16[32,64,128]{2,1,0:T(8,128)(2,1)} %copy-done.6), custom_call_target="tpu_custom_call" | custom-call | flops 100000000 | bytes 41943040 | tf_op jit(solution)/shard_map/returned_rows/pallas_call | solution.py:493
  (8 shorter events, 0.0 us)
Async XLA Ops:
  8.2 48.8 %copy-start.2 = (bf16[4096,128]{1,0:T(8,128)(2,1)S(1)}, bf16[4096,128]{1,0:T(8,128)(2,1)}, u32[]{:S(2)}) copy-start(bf16[4096,128]{1,0:T(8,128)(2,1)} %feat_ref.1) | copy-start | bytes 3145732
  52.8 16.0 %copy-start = (bf16[128,72,128]{2,1,0:T(8,128)(2,1)}, bf16[128,72,128]{2,1,0:T(8,128)(2,1)S(1)}, u32[]{:S(2)}) copy-start(bf16[128,72,128]{2,1,0:T(8,128)(2,1)S(1)} %all_to_all.10.near_ref.names_ref) | copy-start | bytes 7077892
  52.8 16.0 %collective-permute-start = (bf16[128,72,128]{2,1,0:T(8,128)(2,1)S(1)}, bf16[128,72,128]{2,1,0:T(8,128)(2,1)}, u32[]{:S(2)}, u32[]{:S(2)}) collective-permute-start(bf16[128,72,128]{2,1,0:T(8,128)(2,1)S(1)} %all_to_all.10.near_ref.names_ref), channel_id=1, source_target_pairs={{0,1},{1,0},{2,3},{3,2},{4,5},{5,4},{6,7},{7,6},{8,9},{9,8},{10,11... | collective-permute-start | bytes 7077896 | tf_op jit(solution)/shard_map/ppermute | solution.py:530
  57.1 0.7 copy-start.8
  57.8 0.7 copy-start.11
  62.5 1.4 copy-start.1
  63.9 4.9 %copy-start.4 = (bf16[32,128,256]{2,1,0:T(8,128)(2,1)S(1)}, bf16[32,128,256]{2,1,0:T(8,128)(2,1)}, u32[]{:S(2)}) copy-start(bf16[32,128,256]{2,1,0:T(8,128)(2,1)} %get-tuple-element.15.hot_ref) | copy-start | bytes 6291460
  63.9 4.9 %copy-start.5 = (bf16[4096,128]{1,0:T(8,128)(2,1)S(1)}, bf16[4096,128]{1,0:T(8,128)(2,1)}, u32[]{:S(2)}) copy-start(bf16[4096,128]{1,0:T(8,128)(2,1)} %param.14) | copy-start | bytes 3145732
  63.9 4.9 %copy-start.9 = (s32[1,768]{1,0:T(1,128)S(1)}, s32[1,768]{1,0:T(1,128)}, u32[]{:S(2)}) copy-start(s32[1,768]{1,0:T(1,128)} %get-tuple-element.13.list_ref) | copy-start | bytes 9220
  63.9 4.9 %copy-start.10 = (bf16[128,128]{1,0:T(8,128)(2,1)S(1)}, bf16[128,128]{1,0:T(8,128)(2,1)}, u32[]{:S(2)}) copy-start(bf16[128,128]{1,0:T(8,128)(2,1)} %weight_ref.1) | copy-start | bytes 98308
  63.9 4.9 %copy-start.12 = (s32[1,128]{1,0:T(1,128)S(1)}, s32[1,128]{1,0:T(1,128)}, u32[]{:S(2)}) copy-start(s32[1,128]{1,0:T(1,128)} %get-tuple-element.14.group_ref) | copy-start | bytes 1540
  63.9 4.9 %copy-start.13 = (f32[128]{0:T(128)S(1)}, f32[128]{0:T(128)}, u32[]{:S(2)}) copy-start(f32[128]{0:T(128)} %param.13) | copy-start | bytes 1540
  86.5 43.3 %all-to-all-start.1 = ((bf16[128,64,128]{2,1,0:T(8,128)(2,1)}), bf16[128,64,128]{2,1,0:T(8,128)(2,1)S(1)}, u32[]{:S(2)}, u32[]{:S(2)}) async-start(bf16[128,64,128]{2,1,0:T(8,128)(2,1)} %get-tuple-element.19), calls=%async_computation.1 | async-start | bytes 4194304 | tf_op jit(solution)/shard_map/all_to_all | solution.py:533
  99.2 30.6 %copy-start.7 = (s32[1,128,32]{1,2,0:T(8,128)S(1)}, s32[1,128,32]{1,2,0:T(8,128)}, u32[]{:S(2)}) copy-start(s32[1,128,32]{1,2,0:T(8,128)} %param.18) | copy-start | bytes 49156
  106.7 1.3 copy-start.3
  108.0 0.8 copy-start.6
where the time goes:
time: 140 us; the launch traced here: 139 us
  Pallas kernels  54.6 us (39%)
  blocking collectives  44.6 us (32%)
  waiting for transfers between devices  21 us (15%)
  starting transfers between devices  12.7 us (9%)
  local copies, waits for them, and re-layouts  4.88 us (3%)
  between operations  1.44 us (1%)
    all_to_all x1, blocking collectives, body(): lax.all_to_all(outgoing, 'dom', split_axis=0, concat_axis=0, tiled=True)  44.6 us
    all_to_all x1, waiting for transfers between devices, body(): lax.all_to_all(grads, 'dom', split_axis=0, concat_axis=0, tiled=True)  21 us
    pallas_call x1, Pallas kernels, middle(): pl.pallas_call(middle_kernel, name='middle', in_specs=[whole(SMEM)] * 2 +...  17.6 us
    all_to_all x1, starting transfers between devices, body(): lax.all_to_all(grads, 'dom', split_axis=0, concat_axis=0, tiled=True)  12.7 us
    pallas_call x1, Pallas kernels, returned_rows(): pl.pallas_call(returned_kernel, name='returned_rows', in_specs=[whole(SME...  9.42 us
    pallas_call x1, Pallas kernels, outgoing_rows(): pl.pallas_call(outgoing_kernel, name='outgoing_rows', grid=(steps,), in_s...  7.6 us
    pallas_call x1, Pallas kernels, own_backward(): pl.pallas_call(own_backward_kernel, name='own_backward', in_specs=[whole(...  7.45 us
    unnamed x28, local copies, waits for them, and re-layouts  4.88 us
  transfers between devices with their start and end apart: 2, of which 1 were waited for; matrix products, arithmetic and copies ran while one was open for 0% of the time, Pallas kernels for 14%

commit v1 on v0

--- a/solution.py
+++ b/solution.py
@@ -14,7 +14,7 @@
 BF16 = jnp.bfloat16
 I32 = jnp.int32
 PAIRS = 8
-CHAINS = 6
+CHAINS = 4
 NT = (((1,), (1,)), ((), ()))
 
 
@@ -30,58 +30,58 @@
     return pltpu.with_memory_space_constraint(array, pltpu.HBM)
 
 
-def outgoing_kernel(send_ref, feat_ref, hub_ref, wanted_ref, out_ref, wide, stage, names):
-    step = pl.program_id(0)
-    chunk = out_ref.shape[0]
-    rows = send_ref.shape[0]
+def outgoing_kernel(send_ref, feat_ref, hub_ref, wanted_ref, out_ref, wide, stage, names, parcel, sems):
+    rows, parties = send_ref.shape
     width = feat_ref.shape[1]
     half = hub_ref.shape[0] // 2
-
-    @pl.when(step == 0)
-    def _():
-        wide[...] = feat_ref[...].astype(F32)
-        tall = jnp.concatenate([wanted_ref[...].astype(F32)] * (width // rows), axis=0)
-        names[...] = jnp.transpose(tall)
+    wide[...] = feat_ref[...].astype(F32)
+    tall = jnp.concatenate([wanted_ref[...].astype(F32)] * (width // rows), axis=0)
+    names[...] = jnp.transpose(tall)
+
+    @pl.loop(0, rows)
+    def _(j):
+        for q in range(parties):
+            stage[q, pl.ds(j, 1), :] = wide[pl.ds(send_ref[j, q], 1), :]
 
     halves = (hub_ref[:half, :], hub_ref[half:, :])
-
-    @pl.loop(0, chunk // 2)
-    def _(pair):
-        for side in range(2):
-            q = pair * 2 + side
-            for j in range(rows):
-                row = send_ref[j, step * chunk + q]
-                stage[side, pl.ds(j, 1), :] = wide[pl.ds(row, 1), :]
-        for side in range(2):
-            q = pair * 2 + side
-            out_ref[q, 0:rows, :] = stage[side].astype(BF16)
-            out_ref[q, rows : rows + half, :] = halves[side]
-            line = names[pl.ds(step * chunk + q, 1), :]
-            out_ref[q, rows + half :, :] = jnp.broadcast_to(line, (8, width)).astype(BF16)
+    turns = sems.shape[0]
+    chunk = parties // turns
+
+    def send(turn):
+        part = pl.ds(turn * chunk, chunk)
+        return pltpu.make_async_copy(parcel.at[part], out_ref.at[part], sems.at[turn])
+
+    @pl.loop(0, turns)
+    def _(turn):
+        for i in range(chunk):
+            q = turn * chunk + i
+            parcel[q, 0:rows, :] = stage[q].astype(BF16)
+            parcel[q, rows : rows + half, :] = halves[i % 2]
+            line = names[pl.ds(q, 1), :]
+            parcel[q, rows + half :, :] = jnp.broadcast_to(line, (8, width)).astype(BF16)
+        send(turn).start()
+
+    @pl.loop(0, turns)
+    def _(turn):
+        send(turn).wait()
 
 
 def outgoing_rows(send, features, hubs, wanted):
     rows, parties = send.shape
     width = features.shape[1]
     total = rows + hubs.shape[0] // 2 + 8
-    steps = 4
-    chunk = parties // steps
     return pl.pallas_call(
         outgoing_kernel,
         name="outgoing_rows",
-        grid=(steps,),
-        in_specs=[
-            whole(SMEM),
-            pl.BlockSpec(features.shape, lambda i: (0, 0)),
-            pl.BlockSpec(hubs.shape, lambda i: (0, 0)),
-            pl.BlockSpec(wanted.shape, lambda i: (0, 0)),
-        ],
-        out_specs=pl.BlockSpec((chunk, total, width), lambda i: (i, 0, 0)),
-        out_shape=jax.ShapeDtypeStruct((parties, total, width), BF16),
+        in_specs=[whole(SMEM)] + [whole(VMEM)] * 3,
+        out_specs=whole(pltpu.HBM),
+        out_shape=pltpu.HBM((parties, total, width), BF16),
         scratch_shapes=[
             VMEM(features.shape, F32),
-            VMEM((2, rows, width), F32),
+            VMEM((parties, rows, width), F32),
             VMEM((parties, width), F32),
+            VMEM((parties, total, width), BF16),
+            pltpu.SemaphoreType.DMA((16,)),
         ],
         compiler_params=params(60),
         cost_estimate=pl.CostEstimate(flops=0, bytes_accessed=30 << 20, transcendentals=0),
@@ -318,10 +318,10 @@
         list_ref, group_ref[0, 2], 0, hub_turns, tiles_ref, store, sems, forward_body(total, table, 2 * blocks)
     )
 
-    @pl.loop(0, blocks // 4)
-    def _(turn):
-        for i in range(4):
-            b = turn * 4 + i
+    @pl.loop(0, blocks // 2)
+    def _(turn):
+        for i in range(2):
+            b = turn * 2 + i
             preact = jnp.dot(total[b].astype(BF16), weight, preferred_element_type=F32) + bias_ref[...]
             sigmoid = 0.5 * jnp.tanh(0.5 * preact) + 0.5
             act_ref[b] = (preact * sigmoid).astype(BF16)
@@ -452,31 +452,47 @@
     )(lists, groups, in_hbm(back), arrived, in_hbm(tiles))
 
 
-def returned_kernel(send_ref, own_ref, back_ref, hot_ref, sal_ref, hub_ref, stage, hot, chains, sems):
+def returned_kernel(send_ref, own_ref, back_ref, hot_ref, sal_out, hub_ref, stage, hot, first, chains, sems):
     rows, parties = send_ref.shape
     blocks, _, width = hot_ref.shape
     group = parties // blocks
-    own_copy = pltpu.make_async_copy(own_ref, sal_ref, sems.at[0])
+    own_copy = pltpu.make_async_copy(own_ref, first, sems.at[0])
     hot_copy = pltpu.make_async_copy(hot_ref, hot, sems.at[1])
     own_copy.start()
     hot_copy.start()
     for chain in chains:
         chain[...] = jnp.zeros_like(chain)
+
+    @pl.loop(0, parties // 4)
+    def _(turn):
+        for i in range(4):
+            stage[turn * 4 + i] = back_ref[turn * 4 + i, 0:rows, :].astype(F32)
+
     own_copy.wait()
-    sums = (sal_ref,) + tuple(chains)
-
-    @pl.loop(0, parties)
-    def _(q):
-        stage[...] = back_ref[q, 0:rows, :].astype(F32)
-        for j in range(rows):
-            chain = sums[j % len(sums)]
+    sums = (first,) + tuple(chains)
+
+    @pl.loop(0, rows)
+    def _(j):
+        for q in range(parties):
+            chain = sums[q % len(sums)]
             row = send_ref[j, q]
-            chain[pl.ds(row, 1), :] += stage[pl.ds(j, 1), :]
-
-    total = sal_ref[...]
-    for chain in chains:
-        total = total + chain[...]
-    sal_ref[...] = total
+            chain[pl.ds(row, 1), :] += stage[q, pl.ds(j, 1), :]
+
+    turns = sems.shape[0] - 2
+    size = first.shape[0] // turns
+
+    def result(turn):
+        part = pl.ds(turn * size, size)
+        return pltpu.make_async_copy(first.at[part], sal_out.at[part], sems.at[turn + 2])
+
+    @pl.loop(0, turns)
+    def _(turn):
+        part = pl.ds(turn * size, size)
+        total = first[part, :]
+        for chain in chains:
+            total = total + chain[part, :]
+        first[part, :] = total
+        result(turn).start()
 
     hot_copy.wait()
     total = jnp.zeros(hub_ref.shape, F32)
@@ -486,24 +502,29 @@
         total += jnp.dot(pair, grads, preferred_element_type=F32)
     hub_ref[...] = total
 
+    @pl.loop(0, turns)
+    def _(turn):
+        result(turn).wait()
+
 
 def returned_rows(send, own, returned, hot):
-    rows, _ = send.shape
+    rows, parties = send.shape
     own_rows, width = own.shape
     return pl.pallas_call(
         returned_kernel,
         name="returned_rows",
         in_specs=[whole(SMEM), whole(pltpu.HBM), whole(VMEM), whole(pltpu.HBM)],
-        out_specs=[whole(VMEM)] * 2,
+        out_specs=[whole(pltpu.HBM), whole(VMEM)],
         out_shape=[
-            jax.ShapeDtypeStruct((own_rows, width), F32),
+            pltpu.HBM((own_rows, width), F32),
             jax.ShapeDtypeStruct((hot.shape[1], width), F32),
         ],
         scratch_shapes=[
-            VMEM((rows, width), F32),
+            VMEM((parties, rows, width), F32),
             VMEM(hot.shape, BF16),
+            VMEM((own_rows, width), F32),
             [VMEM((own_rows, width), F32)] * (CHAINS - 1),
-            pltpu.SemaphoreType.DMA((2,)),
+            pltpu.SemaphoreType.DMA((2 + 16,)),
         ],
         compiler_params=params(32),
         cost_estimate=pl.CostEstimate(flops=10**8, bytes_accessed=40 << 20, transcendentals=0),

time: 140 us -> 140 us (level)
  no operation moved by 1% of the time
where the time goes in v1:
time: 140 us
  Pallas kernels  54.9 us (39%)
  blocking collectives  44.6 us (32%)
  waiting for transfers between devices  21 us (15%)
  starting transfers between devices  12.7 us (9%)
  local copies, waits for them, and re-layouts  4.88 us (3%)
  between operations  1.46 us (1%)
    all_to_all x1, blocking collectives, body(): lax.all_to_all(outgoing, 'dom', split_axis=0, concat_axis=0, tiled=True)  44.6 us
    all_to_all x1, waiting for transfers between devices, body(): lax.all_to_all(grads, 'dom', split_axis=0, concat_axis=0, tiled=True)  21 us
    pallas_call x1, Pallas kernels, middle(): pl.pallas_call(middle_kernel, name='middle', in_specs=[whole(SMEM)] * 2 +...  18.7 us
    all_to_all x1, starting transfers between devices, body(): lax.all_to_all(grads, 'dom', split_axis=0, concat_axis=0, tiled=True)  12.7 us
    pallas_call x1, Pallas kernels, returned_rows(): pl.pallas_call(returned_kernel, name='returned_rows', in_specs=[whole(SME...  9.85 us
    pallas_call x1, Pallas kernels, own_backward(): pl.pallas_call(own_backward_kernel, name='own_backward', in_specs=[whole(...  7.45 us
    pallas_call x1, Pallas kernels, outgoing_rows(): pl.pallas_call(outgoing_kernel, name='outgoing_rows', in_specs=[whole(SME...  6.42 us
    unnamed x28, local copies, waits for them, and re-layouts  4.88 us
  transfers between devices with their start and end apart: 2, of which 1 were waited for; matrix products, arithmetic and copies ran while one was open for 0% of the time, Pallas kernels for 14%

profile of v1, /device:TPU:0, one launch (start us, length us, event | category | flops | bytes accessed | tf_op | source)
XLA Modules:
  0.0 139.5 jit_solution(5179547966761948692)
XLA Ops:
  0.6 6.4 %outgoing_rows.1 = bf16[128,72,128]{2,1,0:T(8,128)(2,1)} custom-call(s32[32,128]{1,0:T(8,128)} %bitcast.16, bf16[4096,128]{1,0:T(8,128)(2,1)} %feat_ref.1, bf16[64,128]{1,0:T(8,128)(2,1)} %hub_ref.1, s32[32,128]{1,0:T(8,128)} %bitcast.19), custom_call_target="tpu_custom_call" | custom-call | bytes 31457280 | tf_op jit(solution)/shard_map/outgoing_rows/pallas_call | solution.py:73
  7.1 0.0 copy-start.2
  7.1 44.6 %all_to_all.10.near_ref.names_ref = bf16[128,72,128]{2,1,0:T(8,128)(2,1)S(1)} all-to-all(bf16[128,72,128]{2,1,0:T(8,128)(2,1)} %outgoing_rows.1), channel_id=1, replica_groups=mesh['dom'=128] {'dom'}, dimensions={0} | all-to-all | bytes 4718592 | tf_op jit(solution)/shard_map/all_to_all | solution.py:548
  51.7 0.0 collective-permute-start
  52.3 3.6 %plan.1 = (s32[1,768]{1,0:T(1,128)}, s32[1,128]{1,0:T(1,128)}, bf16[32,128,256]{2,1,0:T(8,128)(2,1)}) custom-call(s32[1]{0:T(128)S(6)} %copy.13.count_ref, s32[1]{0:T(128)} %bitcast.side_ref, s32[2,512]{1,0:T(2,128)} %bitcast.22, s32[32,128]{1,0:T(8,128)} %bitcast.20), custom_call_target="tpu_custom_call" | custom-call | flops 10000000 | bytes 8388608 | tf_op jit(solution)/shard_map/plan/pallas_call | solution.py:154
  55.9 0.0 copy-done.2
  55.9 0.7 copy-done.8
  56.6 0.7 copy-done.11
  57.3 4.1 %own_forward.1.start_ref = f32[32,128,128]{2,1,0:T(8,128)S(1)} custom-call(s32[1,768]{1,0:T(1,128)S(1)} %copy-done.8, s32[1,128]{1,0:T(1,128)S(1)} %copy-done.11, bf16[32,128,128]{2,1,0:T(8,128)(2,1)S(1)} %bitcast.13, bf16[512,128,128]{2,1,0:T(8,128)(2,1)} %tiles_ref.7), custom_call_target="tpu_custom_call" | custom-call | flops 1000000000 | bytes 41943040 | tf_op jit(solution)/shard_map/own_forward/pallas_call | solution.py:248
  61.4 0.0 copy-start.1
  61.4 1.4 copy-done.1
  62.8 0.0 copy-start.12
  62.8 0.0 copy-start.13
  62.8 4.8 %boundary_forward.1.start_ref = f32[32,128,128]{2,1,0:T(8,128)S(1)} custom-call(s32[1,768]{1,0:T(1,128)S(1)} %copy-done.8, s32[1,128]{1,0:T(1,128)S(1)} %copy-done.11, bf16[128,72,128]{2,1,0:T(8,128)(2,1)S(1)} %all_to_all.10.near_ref.names_ref, f32[32,128,128]{2,1,0:T(8,128)} %copy-done.1, bf16[512,128,128]{2,1,0:T(8,128)(2,1)} %tiles_ref.7), custom_call_target="tpu_custom_call" | custom-call | flops 1000000000 | bytes 41943040 | tf_op jit(solution)/shard_map/boundary_forward/pallas_call | solution.py:280
  67.6 0.0 collective-permute-done.far_ref
  67.6 0.0 copy-done
  67.6 0.0 copy-done.4
  67.6 0.0 copy-done.5
  67.6 0.0 copy-done.9
  67.6 0.0 copy-done.10
  67.7 0.0 copy-done.12
  67.7 0.0 copy-done.13
  67.7 18.7 %middle.1 = (bf16[32,128,128]{2,1,0:T(8,128)(2,1)}, bf16[32,128,128]{2,1,0:T(8,128)(2,1)}, bf16[128,64,128]{2,1,0:T(8,128)(2,1)}) custom-call(s32[1,768]{1,0:T(1,128)S(1)} %copy-done.9, s32[1,128]{1,0:T(1,128)S(1)} %copy-done.12, bf16[128,72,128]{2,1,0:T(8,128)(2,1)S(1)} %all_to_all.10.near_ref.names_ref, ...), custom_call_target="tpu_custom_call" | custom-call | flops 4000000000 | bytes 62914560 | tf_op jit(solution)/shard_map/middle/pallas_call | solution.py:375
  86.4 12.7 %all-to-all-start.1 = ((bf16[128,64,128]{2,1,0:T(8,128)(2,1)}), bf16[128,64,128]{2,1,0:T(8,128)(2,1)S(1)}, u32[]{:S(2)}, u32[]{:S(2)}) async-start(bf16[128,64,128]{2,1,0:T(8,128)(2,1)} %get-tuple-element.19), calls=%async_computation.1 | async-start | bytes 4194304 | tf_op jit(solution)/shard_map/all_to_all | solution.py:554
  99.1 0.0 copy-start.7
  99.1 7.4 %own_backward.1 = (f32[32,128,128]{2,1,0:T(8,128)S(1)}, bf16[32,64,128]{2,1,0:T(8,128)(2,1)S(1)}) custom-call(s32[1,768]{1,0:T(1,128)S(1)} %copy-done.9, s32[1,128]{1,0:T(1,128)S(1)} %copy-done.12, bf16[32,128,128]{2,1,0:T(8,128)(2,1)} %get-tuple-element.17.back_ref, bf16[128,72,128]{2,1,0:T(8,128)(2,1)} %copy-done, bf16[512,128,128]{2,1,0:T(8,128)(2,1)} %tiles_ref.7), custom_call_target="tpu_custom_call" | custom-call | flops 1000000000 | bytes 41943040 | tf_op jit(solution)/shard_map/own_backward/pallas_call | solution.py:438
  106.5 0.0 copy-start.3
  106.6 1.3 copy-done.3
  107.9 0.8 copy-done.6
  108.7 21.0 %all-to-all-done.1.back_ref = bf16[128,64,128]{2,1,0:T(8,128)(2,1)S(1)} async-done(((bf16[128,64,128]{2,1,0:T(8,128)(2,1)}), bf16[128,64,128]{2,1,0:T(8,128)(2,1)S(1)}, u32[]{:S(2)}, u32[]{:S(2)}) %all-to-all-start.1) | async-done | bytes 2097184 | tf_op jit(solution)/shard_map/all_to_all | solution.py:554
  129.7 0.0 copy-done.7
  129.7 9.9 %returned_rows.1 = (f32[4096,128]{1,0:T(8,128)}, f32[64,128]{1,0:T(8,128)}) custom-call(s32[32,128]{1,0:T(8,128)S(1)} %bitcast.17, f32[4096,128]{1,0:T(8,128)} %bitcast.14, bf16[128,64,128]{2,1,0:T(8,128)(2,1)S(1)} %all-to-all-done.1.back_ref, bf16[32,64,128]{2,1,0:T(8,128)(2,1)} %copy-done.6), custom_call_target="tpu_custom_call" | custom-call | flops 100000000 | bytes 41943040 | tf_op jit(solution)/shard_map/returned_rows/pallas_call | solution.py:513
  (8 shorter events, 0.0 us)
Async XLA Ops:
  7.1 48.9 %copy-start.2 = (bf16[4096,128]{1,0:T(8,128)(2,1)S(1)}, bf16[4096,128]{1,0:T(8,128)(2,1)}, u32[]{:S(2)}) copy-start(bf16[4096,128]{1,0:T(8,128)(2,1)} %feat_ref.1) | copy-start | bytes 3145732
  51.6 16.0 %copy-start = (bf16[128,72,128]{2,1,0:T(8,128)(2,1)}, bf16[128,72,128]{2,1,0:T(8,128)(2,1)S(1)}, u32[]{:S(2)}) copy-start(bf16[128,72,128]{2,1,0:T(8,128)(2,1)S(1)} %all_to_all.10.near_ref.names_ref) | copy-start | bytes 7077892
  51.7 15.9 %collective-permute-start = (bf16[128,72,128]{2,1,0:T(8,128)(2,1)S(1)}, bf16[128,72,128]{2,1,0:T(8,128)(2,1)}, u32[]{:S(2)}, u32[]{:S(2)}) collective-permute-start(bf16[128,72,128]{2,1,0:T(8,128)(2,1)S(1)} %all_to_all.10.near_ref.names_ref), channel_id=1, source_target_pairs={{0,1},{1,0},{2,3},{3,2},{4,5},{5,4},{6,7},{7,6},{8,9},{9,8},{10,11... | collective-permute-start | bytes 7077896 | tf_op jit(solution)/shard_map/ppermute | solution.py:551
  55.9 0.7 copy-start.8
  56.6 0.7 copy-start.11
  61.4 1.4 copy-start.1
  62.7 4.9 %copy-start.4 = (bf16[32,128,256]{2,1,0:T(8,128)(2,1)S(1)}, bf16[32,128,256]{2,1,0:T(8,128)(2,1)}, u32[]{:S(2)}) copy-start(bf16[32,128,256]{2,1,0:T(8,128)(2,1)} %get-tuple-element.15.hot_ref) | copy-start | bytes 6291460
  62.7 4.9 %copy-start.5 = (bf16[4096,128]{1,0:T(8,128)(2,1)S(1)}, bf16[4096,128]{1,0:T(8,128)(2,1)}, u32[]{:S(2)}) copy-start(bf16[4096,128]{1,0:T(8,128)(2,1)} %param.14) | copy-start | bytes 3145732
  62.7 4.9 %copy-start.9 = (s32[1,768]{1,0:T(1,128)S(1)}, s32[1,768]{1,0:T(1,128)}, u32[]{:S(2)}) copy-start(s32[1,768]{1,0:T(1,128)} %get-tuple-element.13.list_ref) | copy-start | bytes 9220
  62.7 4.9 %copy-start.10 = (bf16[128,128]{1,0:T(8,128)(2,1)S(1)}, bf16[128,128]{1,0:T(8,128)(2,1)}, u32[]{:S(2)}) copy-start(bf16[128,128]{1,0:T(8,128)(2,1)} %weight_ref.1) | copy-start | bytes 98308
  62.8 4.9 %copy-start.12 = (s32[1,128]{1,0:T(1,128)S(1)}, s32[1,128]{1,0:T(1,128)}, u32[]{:S(2)}) copy-start(s32[1,128]{1,0:T(1,128)} %get-tuple-element.14.group_ref) | copy-start | bytes 1540
  62.8 4.9 %copy-start.13 = (f32[128]{0:T(128)S(1)}, f32[128]{0:T(128)}, u32[]{:S(2)}) copy-start(f32[128]{0:T(128)} %param.13) | copy-start | bytes 1540
  86.4 43.3 %all-to-all-start.1 = ((bf16[128,64,128]{2,1,0:T(8,128)(2,1)}), bf16[128,64,128]{2,1,0:T(8,128)(2,1)S(1)}, u32[]{:S(2)}, u32[]{:S(2)}) async-start(bf16[128,64,128]{2,1,0:T(8,128)(2,1)} %get-tuple-element.19), calls=%async_computation.1 | async-start | bytes 4194304 | tf_op jit(solution)/shard_map/all_to_all | solution.py:554
  99.1 30.6 %copy-start.7 = (s32[1,128,32]{1,2,0:T(8,128)S(1)}, s32[1,128,32]{1,2,0:T(8,128)}, u32[]{:S(2)}) copy-start(s32[1,128,32]{1,2,0:T(8,128)} %param.18) | copy-start | bytes 49156
  106.5 1.3 copy-start.3
  107.9 0.8 copy-start.6

commit v2 on v1

--- a/solution.py
+++ b/solution.py
@@ -14,7 +14,9 @@
 BF16 = jnp.bfloat16
 I32 = jnp.int32
 PAIRS = 8
-CHAINS = 4
+CHAINS = 8
+ACT = 8
+TURNS = 16
 NT = (((1,), (1,)), ((), ()))
 
 
@@ -259,50 +261,48 @@
 
 
 def boundary_forward_kernel(
-    list_ref, group_ref, near_ref, start_ref, tiles_ref, sum_ref, table, total, store, sems, start_sem
+    list_ref, group_ref, near_ref, tiles_ref, sum_ref, table, total, store, sems
 ):
     blocks, tile, width = sum_ref.shape
     group = near_ref.shape[0] // blocks
     begin, turns = group_ref[0, 1], group_ref[0, 4]
-    start_copy = pltpu.make_async_copy(start_ref, total.at[pl.ds(0, blocks)], start_sem)
-    start_copy.start()
     fetch_tiles(list_ref, begin, 0, turns, tiles_ref, store, sems)
+    total[...] = jnp.zeros_like(total)
     for b in range(blocks):
         table[b] = near_ref[b * group : (b + 1) * group, 0 : tile // group, :].reshape(tile, width)
     table[blocks] = jnp.zeros(table.shape[1:], BF16)
-    start_copy.wait()
     tile_loop(list_ref, begin, 0, turns, tiles_ref, store, sems, forward_body(total, table, blocks))
     sum_ref[...] = total[:blocks]
 
 
-def boundary_forward(lists, groups, arrived, start, tiles):
-    blocks, tile, width = start.shape
+def boundary_forward(lists, groups, arrived, blocks, tiles):
+    tile, width = tiles.shape[1], arrived.shape[2]
     return pl.pallas_call(
         boundary_forward_kernel,
         name="boundary_forward",
-        in_specs=[whole(SMEM)] * 2 + [whole(VMEM), whole(pltpu.HBM), whole(pltpu.HBM)],
+        in_specs=[whole(SMEM)] * 2 + [whole(VMEM), whole(pltpu.HBM)],
         out_specs=whole(VMEM),
-        out_shape=jax.ShapeDtypeStruct(start.shape, F32),
+        out_shape=jax.ShapeDtypeStruct((blocks, tile, width), F32),
         scratch_shapes=[VMEM((blocks + 1, tile, width), BF16), VMEM((blocks + 1, tile, width), F32)]
-        + store_scratch(tiles, blocks)
-        + [pltpu.SemaphoreType.DMA],
+        + store_scratch(tiles, blocks),
         compiler_params=params(40),
         cost_estimate=pl.CostEstimate(flops=10**9, bytes_accessed=40 << 20, transcendentals=0),
-    )(lists, groups, arrived, in_hbm(start), in_hbm(tiles))
+    )(lists, groups, arrived, in_hbm(tiles))
 
 
 def middle_kernel(
-    list_ref, group_ref, near_ref, far_ref, hot_ref, start_ref, weight_ref, bias_ref, cot_ref, tiles_ref,
+    list_ref, group_ref, near_ref, far_ref, hot_ref, start_ref, part_ref, weight_ref, bias_ref, cot_ref, tiles_ref,
     act_out, back_out, grads_ref, act_ref, table, total, swapped, spread, parcel, store, sems, out_sems,
 ):
     blocks, tile, width = act_ref.shape
     group = near_ref.shape[0] // blocks
     rows = tile // group
     weight = weight_ref[...]
+    start_copy = pltpu.make_async_copy(start_ref, total.at[pl.ds(0, blocks)], out_sems.at[blocks // 2])
+    start_copy.start()
     near_turns, hub_turns = group_ref[0, 4], group_ref[0, 5]
     fetch_tiles(list_ref, group_ref[0, 2], 0, hub_turns, tiles_ref, store, sems)
     fetch_tiles(list_ref, group_ref[0, 1] - hub_turns, hub_turns, hub_turns + near_turns, tiles_ref, store, sems)
-    total[:blocks] = start_ref[...]
 
     @pl.loop(0, blocks // 4)
     def _(turn):
@@ -313,15 +313,17 @@
             picked = jnp.dot(hot_ref[b], jnp.concatenate([near, far], axis=0), preferred_element_type=F32)
             table[b] = picked.astype(BF16)
 
+    start_copy.wait()
+    total[:blocks] += part_ref[...]
     table[blocks] = jnp.zeros(table.shape[1:], BF16)
     tile_loop(
         list_ref, group_ref[0, 2], 0, hub_turns, tiles_ref, store, sems, forward_body(total, table, 2 * blocks)
     )
 
-    @pl.loop(0, blocks // 2)
-    def _(turn):
-        for i in range(2):
-            b = turn * 2 + i
+    @pl.loop(0, blocks // ACT)
+    def _(turn):
+        for i in range(ACT):
+            b = turn * ACT + i
             preact = jnp.dot(total[b].astype(BF16), weight, preferred_element_type=F32) + bias_ref[...]
             sigmoid = 0.5 * jnp.tanh(0.5 * preact) + 0.5
             act_ref[b] = (preact * sigmoid).astype(BF16)
@@ -368,7 +370,7 @@
         result.wait()
 
 
-def middle(lists, groups, arrived, other, hot, start, weight, bias, cotangent, tiles):
+def middle(lists, groups, arrived, other, hot, start, near, weight, bias, cotangent, tiles):
     blocks, tile, width = start.shape
     parties = arrived.shape[0]
     rows = blocks * tile // parties
@@ -376,7 +378,9 @@
         middle_kernel,
         name="middle",
         in_specs=[whole(SMEM)] * 2
-        + [whole(VMEM)] * 7
+        + [whole(VMEM)] * 3
+        + [whole(pltpu.HBM)]
+        + [whole(VMEM)] * 4
         + [whole(pltpu.HBM)],
         out_specs=[whole(pltpu.HBM)] * 3,
         out_shape=[
@@ -397,7 +401,7 @@
         compiler_params=params(42),
         cost_estimate=pl.CostEstimate(flops=4 * 10**9, bytes_accessed=60 << 20, transcendentals=10**6),
     )(
-        lists, groups, arrived, other, hot, start, weight, bias, cotangent.reshape(blocks, tile, width), in_hbm(tiles)
+        lists, groups, arrived, other, hot, in_hbm(start), near, weight, bias, cotangent.reshape(blocks, tile, width), in_hbm(tiles)
     )
 
 
@@ -524,7 +528,7 @@
             VMEM(hot.shape, BF16),
             VMEM((own_rows, width), F32),
             [VMEM((own_rows, width), F32)] * (CHAINS - 1),
-            pltpu.SemaphoreType.DMA((2 + 16,)),
+            pltpu.SemaphoreType.DMA((2 + TURNS,)),
         ],
         compiler_params=params(32),
         cost_estimate=pl.CostEstimate(flops=10**8, bytes_accessed=40 << 20, transcendentals=0),
@@ -549,8 +553,10 @@
     lists, groups, hot = plan(tile_count, side, tile_blocks.T, wanted, blocks, tile)
     start = own_forward(lists, groups, features, tiles)
     other = lax.ppermute(arrived, "dom", pairs)
-    start = boundary_forward(lists, groups, arrived, start, tiles)
-    act, back, grads = middle(lists, groups, arrived, other, hot, start, weight, bias.reshape(1, -1), cotangent, tiles)
+    near = boundary_forward(lists, groups, arrived, blocks, tiles)
+    act, back, grads = middle(
+        lists, groups, arrived, other, hot, start, near, weight, bias.reshape(1, -1), cotangent, tiles
+    )
     returned = lax.all_to_all(grads, "dom", split_axis=0, concat_axis=0, tiled=True)
     own, hub_hot = own_backward(lists, groups, back, arrived, tiles, hubs.shape[0])
     saliency, hub_saliency = returned_rows(send, own.reshape(own_rows, width), returned, hub_hot)

time: 140 us -> 137 us (0.979)
  Pallas kernels: 54.9 us -> 52.9 us
    pallas_call x1, Pallas kernels: 18.7 us -> 17.2 us  [middle(): pl.pallas_call(middle_kernel, name='middle', in_specs=[whole(SMEM)] * 2 +...]
  transfers between devices with their start and end apart: 2 -> 2, of which waited for: 1 -> 1; matrix products, arithmetic and copies ran while one was open for 0% -> 0% of each run, Pallas kernels for 14% -> 15%
where the time goes in v2:
time: 137 us; the launch traced here: 136 us
  Pallas kernels  52.9 us (39%)
  blocking collectives  44.6 us (33%)
  waiting for transfers between devices  21 us (15%)
  starting transfers between devices  12.2 us (9%)
  local copies, waits for them, and re-layouts  3.54 us (3%)
  between operations  1.49 us (1%)
    all_to_all x1, blocking collectives, body(): lax.all_to_all(outgoing, 'dom', split_axis=0, concat_axis=0, tiled=True)  44.6 us
    all_to_all x1, waiting for transfers between devices, body(): lax.all_to_all(grads, 'dom', split_axis=0, concat_axis=0, tiled=True)  21 us
    pallas_call x1, Pallas kernels, middle(): pl.pallas_call(middle_kernel, name='middle', in_specs=[whole(SMEM)] * 2 +...  17.2 us
    all_to_all x1, starting transfers between devices, body(): lax.all_to_all(grads, 'dom', split_axis=0, concat_axis=0, tiled=True)  12.2 us
    pallas_call x1, Pallas kernels, returned_rows(): pl.pallas_call(returned_kernel, name='returned_rows', in_specs=[whole(SME...  9.08 us
    pallas_call x1, Pallas kernels, own_backward(): pl.pallas_call(own_backward_kernel, name='own_backward', in_specs=[whole(...  7.48 us
    pallas_call x1, Pallas kernels, outgoing_rows(): pl.pallas_call(outgoing_kernel, name='outgoing_rows', in_specs=[whole(SME...  6.42 us
    pallas_call x1, Pallas kernels, boundary_forward(): pl.pallas_call(boundary_forward_kernel, name='boundary_forward', in_specs...  5 us
  transfers between devices with their start and end apart: 2, of which 1 were waited for; matrix products, arithmetic and copies ran while one was open for 0% of the time, Pallas kernels for 15%

profile of v2, /device:TPU:0, one launch (start us, length us, event | category | flops | bytes accessed | tf_op | source)
XLA Modules:
  0.0 135.7 jit_solution(14394997194330714084)
XLA Ops:
  0.6 6.4 %outgoing_rows.1 = bf16[128,72,128]{2,1,0:T(8,128)(2,1)} custom-call(s32[32,128]{1,0:T(8,128)} %bitcast.16, bf16[4096,128]{1,0:T(8,128)(2,1)} %feat_ref.1, bf16[64,128]{1,0:T(8,128)(2,1)} %hub_ref.1, s32[32,128]{1,0:T(8,128)} %bitcast.19), custom_call_target="tpu_custom_call" | custom-call | bytes 31457280 | tf_op jit(solution)/shard_map/outgoing_rows/pallas_call | solution.py:75
  7.1 0.0 copy-start.2
  7.1 44.6 %all_to_all.10.near_ref.names_ref = bf16[128,72,128]{2,1,0:T(8,128)(2,1)S(1)} all-to-all(bf16[128,72,128]{2,1,0:T(8,128)(2,1)} %outgoing_rows.1), channel_id=1, replica_groups=mesh['dom'=128] {'dom'}, dimensions={0} | all-to-all | bytes 4718592 | tf_op jit(solution)/shard_map/all_to_all | solution.py:552
  51.7 0.0 collective-permute-start
  52.3 3.6 %plan.1 = (s32[1,768]{1,0:T(1,128)}, s32[1,128]{1,0:T(1,128)}, bf16[32,128,256]{2,1,0:T(8,128)(2,1)}) custom-call(s32[1]{0:T(128)S(6)} %copy.13.count_ref, s32[1]{0:T(128)} %bitcast.side_ref, s32[2,512]{1,0:T(2,128)} %bitcast.22, s32[32,128]{1,0:T(8,128)} %bitcast.20), custom_call_target="tpu_custom_call" | custom-call | flops 10000000 | bytes 8388608 | tf_op jit(solution)/shard_map/plan/pallas_call | solution.py:156
  55.9 0.0 copy-done.2
  55.9 0.7 copy-done.8
  56.6 0.7 copy-done.11
  57.3 4.1 %own_forward.1.start_ref = f32[32,128,128]{2,1,0:T(8,128)S(1)} custom-call(s32[1,768]{1,0:T(1,128)S(1)} %copy-done.8, s32[1,128]{1,0:T(1,128)S(1)} %copy-done.11, bf16[32,128,128]{2,1,0:T(8,128)(2,1)S(1)} %bitcast.13, bf16[512,128,128]{2,1,0:T(8,128)(2,1)} %tiles_ref.7), custom_call_target="tpu_custom_call" | custom-call | flops 1000000000 | bytes 41943040 | tf_op jit(solution)/shard_map/own_forward/pallas_call | solution.py:250
  61.4 0.0 copy-start.1
  61.4 0.0 copy-start.3
  61.4 0.0 copy-start.5
  61.4 0.0 copy-start.9
  61.4 0.0 copy-start.10
  61.4 0.0 copy-start.12
  61.4 0.0 copy-start.13
  61.5 5.0 %boundary_forward.1.part_ref = f32[32,128,128]{2,1,0:T(8,128)S(1)} custom-call(s32[1,768]{1,0:T(1,128)S(1)} %copy-done.8, s32[1,128]{1,0:T(1,128)S(1)} %copy-done.11, bf16[128,72,128]{2,1,0:T(8,128)(2,1)S(1)} %all_to_all.10.near_ref.names_ref, bf16[512,128,128]{2,1,0:T(8,128)(2,1)} %tiles_ref.7), custom_call_target="tpu_custom_call" | custom-call | flops 1000000000 | bytes 41943040 | tf_op jit(solution)/shard_map/boundary_forward/pallas_call | solution.py:280
  66.5 0.0 copy-done.1
  66.5 0.0 collective-permute-done.far_ref
  66.5 0.0 copy-done
  66.5 0.0 copy-done.3
  66.5 0.0 copy-done.5
  66.5 0.0 copy-done.9
  66.5 0.0 copy-done.10
  66.6 17.2 %middle.1 = (bf16[32,128,128]{2,1,0:T(8,128)(2,1)}, bf16[32,128,128]{2,1,0:T(8,128)(2,1)}, bf16[128,64,128]{2,1,0:T(8,128)(2,1)}) custom-call(s32[1,768]{1,0:T(1,128)S(1)} %copy-done.9, s32[1,128]{1,0:T(1,128)S(1)} %copy-done.12, bf16[128,72,128]{2,1,0:T(8,128)(2,1)S(1)} %all_to_all.10.near_ref.names_ref, ...), custom_call_target="tpu_custom_call" | custom-call | flops 4000000000 | bytes 62914560 | tf_op jit(solution)/shard_map/middle/pallas_call | solution.py:377
  83.8 12.2 %all-to-all-start.1 = ((bf16[128,64,128]{2,1,0:T(8,128)(2,1)}), bf16[128,64,128]{2,1,0:T(8,128)(2,1)S(1)}, u32[]{:S(2)}, u32[]{:S(2)}) async-start(bf16[128,64,128]{2,1,0:T(8,128)(2,1)} %get-tuple-element.19), calls=%async_computation.1 | async-start | bytes 4194304 | tf_op jit(solution)/shard_map/all_to_all | solution.py:560
  96.0 0.0 copy-start.7
  96.0 7.5 %own_backward.1 = (f32[32,128,128]{2,1,0:T(8,128)S(1)}, bf16[32,64,128]{2,1,0:T(8,128)(2,1)S(1)}) custom-call(s32[1,768]{1,0:T(1,128)S(1)} %copy-done.9, s32[1,128]{1,0:T(1,128)S(1)} %copy-done.12, bf16[32,128,128]{2,1,0:T(8,128)(2,1)} %get-tuple-element.17.back_ref, bf16[128,72,128]{2,1,0:T(8,128)(2,1)} %copy-done, bf16[512,128,128]{2,1,0:T(8,128)(2,1)} %tiles_ref.7), custom_call_target="tpu_custom_call" | custom-call | flops 1000000000 | bytes 41943040 | tf_op jit(solution)/shard_map/own_backward/pallas_call | solution.py:442
  103.5 1.3 copy-done.4
  104.9 0.8 copy-done.6
  105.7 21.0 %all-to-all-done.1.back_ref = bf16[128,64,128]{2,1,0:T(8,128)(2,1)S(1)} async-done(((bf16[128,64,128]{2,1,0:T(8,128)(2,1)}), bf16[128,64,128]{2,1,0:T(8,128)(2,1)S(1)}, u32[]{:S(2)}, u32[]{:S(2)}) %all-to-all-start.1) | async-done | bytes 2097184 | tf_op jit(solution)/shard_map/all_to_all | solution.py:560
  126.6 9.1 %returned_rows.1 = (f32[4096,128]{1,0:T(8,128)}, f32[64,128]{1,0:T(8,128)}) custom-call(s32[32,128]{1,0:T(8,128)S(1)} %bitcast.17, f32[4096,128]{1,0:T(8,128)} %bitcast.14, bf16[128,64,128]{2,1,0:T(8,128)(2,1)S(1)} %all-to-all-done.1.back_ref, bf16[32,64,128]{2,1,0:T(8,128)(2,1)} %copy-done.6), custom_call_target="tpu_custom_call" | custom-call | flops 100000000 | bytes 41943040 | tf_op jit(solution)/shard_map/returned_rows/pallas_call | solution.py:517
  (8 shorter events, 0.0 us)
Async XLA Ops:
  7.1 48.9 %copy-start.2 = (bf16[4096,128]{1,0:T(8,128)(2,1)S(1)}, bf16[4096,128]{1,0:T(8,128)(2,1)}, u32[]{:S(2)}) copy-start(bf16[4096,128]{1,0:T(8,128)(2,1)} %feat_ref.1) | copy-start | bytes 3145732
  51.6 14.8 %copy-start = (bf16[128,72,128]{2,1,0:T(8,128)(2,1)}, bf16[128,72,128]{2,1,0:T(8,128)(2,1)S(1)}, u32[]{:S(2)}) copy-start(bf16[128,72,128]{2,1,0:T(8,128)(2,1)S(1)} %all_to_all.10.near_ref.names_ref) | copy-start | bytes 7077892
  51.7 14.8 %collective-permute-start = (bf16[128,72,128]{2,1,0:T(8,128)(2,1)S(1)}, bf16[128,72,128]{2,1,0:T(8,128)(2,1)}, u32[]{:S(2)}, u32[]{:S(2)}) collective-permute-start(bf16[128,72,128]{2,1,0:T(8,128)(2,1)S(1)} %all_to_all.10.near_ref.names_ref), channel_id=1, source_target_pairs={{0,1},{1,0},{2,3},{3,2},{4,5},{5,4},{6,7},{7,6},{8,9},{9,8},{10,11... | collective-permute-start | bytes 7077896 | tf_op jit(solution)/shard_map/ppermute | solution.py:555
  55.9 0.7 copy-start.8
  56.6 0.7 copy-start.11
  61.4 5.1 %copy-start.1 = (f32[32,128,128]{2,1,0:T(8,128)}, f32[32,128,128]{2,1,0:T(8,128)S(1)}, u32[]{:S(2)}) copy-start(f32[32,128,128]{2,1,0:T(8,128)S(1)} %own_forward.1.start_ref) | copy-start | bytes 6291460
  61.4 5.1 %copy-start.3 = (bf16[32,128,256]{2,1,0:T(8,128)(2,1)S(1)}, bf16[32,128,256]{2,1,0:T(8,128)(2,1)}, u32[]{:S(2)}) copy-start(bf16[32,128,256]{2,1,0:T(8,128)(2,1)} %get-tuple-element.15.hot_ref) | copy-start | bytes 6291460
  61.4 5.1 %copy-start.5 = (bf16[4096,128]{1,0:T(8,128)(2,1)S(1)}, bf16[4096,128]{1,0:T(8,128)(2,1)}, u32[]{:S(2)}) copy-start(bf16[4096,128]{1,0:T(8,128)(2,1)} %param.14) | copy-start | bytes 3145732
  61.4 5.1 %copy-start.9 = (s32[1,768]{1,0:T(1,128)S(1)}, s32[1,768]{1,0:T(1,128)}, u32[]{:S(2)}) copy-start(s32[1,768]{1,0:T(1,128)} %get-tuple-element.13.list_ref) | copy-start | bytes 9220
  61.4 5.1 %copy-start.10 = (bf16[128,128]{1,0:T(8,128)(2,1)S(1)}, bf16[128,128]{1,0:T(8,128)(2,1)}, u32[]{:S(2)}) copy-start(bf16[128,128]{1,0:T(8,128)(2,1)} %weight_ref.1) | copy-start | bytes 98308
  61.4 5.1 %copy-start.12 = (s32[1,128]{1,0:T(1,128)S(1)}, s32[1,128]{1,0:T(1,128)}, u32[]{:S(2)}) copy-start(s32[1,128]{1,0:T(1,128)} %get-tuple-element.14.group_ref) | copy-start | bytes 1540
  61.4 5.1 %copy-start.13 = (f32[128]{0:T(128)S(1)}, f32[128]{0:T(128)}, u32[]{:S(2)}) copy-start(f32[128]{0:T(128)} %param.13) | copy-start | bytes 1540
  83.8 42.8 %all-to-all-start.1 = ((bf16[128,64,128]{2,1,0:T(8,128)(2,1)}), bf16[128,64,128]{2,1,0:T(8,128)(2,1)S(1)}, u32[]{:S(2)}, u32[]{:S(2)}) async-start(bf16[128,64,128]{2,1,0:T(8,128)(2,1)} %get-tuple-element.19), calls=%async_computation.1 | async-start | bytes 4194304 | tf_op jit(solution)/shard_map/all_to_all | solution.py:560
  96.0 30.6 %copy-start.7 = (s32[1,128,32]{1,2,0:T(8,128)S(1)}, s32[1,128,32]{1,2,0:T(8,128)}, u32[]{:S(2)}) copy-start(s32[1,128,32]{1,2,0:T(8,128)} %param.18) | copy-start | bytes 49156
  103.5 1.3 copy-start.4
  104.9 0.8 copy-start.6

commit v3 on v2

--- a/solution.py
+++ b/solution.py
@@ -15,7 +15,7 @@
 I32 = jnp.int32
 PAIRS = 8
 CHAINS = 8
-ACT = 8
+ACT = 16
 TURNS = 16
 NT = (((1,), (1,)), ((), ()))
 
@@ -304,10 +304,10 @@
     fetch_tiles(list_ref, group_ref[0, 2], 0, hub_turns, tiles_ref, store, sems)
     fetch_tiles(list_ref, group_ref[0, 1] - hub_turns, hub_turns, hub_turns + near_turns, tiles_ref, store, sems)
 
-    @pl.loop(0, blocks // 4)
-    def _(turn):
-        for i in range(4):
-            b = turn * 4 + i
+    @pl.loop(0, blocks // 8)
+    def _(turn):
+        for i in range(8):
+            b = turn * 8 + i
             near = near_ref[pl.ds(b * group, group), rows : 2 * rows, :].reshape(tile, width)
             far = far_ref[pl.ds(b * group, group), rows : 2 * rows, :].reshape(tile, width)
             picked = jnp.dot(hot_ref[b], jnp.concatenate([near, far], axis=0), preferred_element_type=F32)
@@ -324,6 +324,8 @@
     def _(turn):
         for i in range(ACT):
             b = turn * ACT + i
+            for part in range(2):
+                spread[2 * b + part] = jnp.zeros(spread.shape[1:], F32)
             preact = jnp.dot(total[b].astype(BF16), weight, preferred_element_type=F32) + bias_ref[...]
             sigmoid = 0.5 * jnp.tanh(0.5 * preact) + 0.5
             act_ref[b] = (preact * sigmoid).astype(BF16)
@@ -337,7 +339,7 @@
     )
     for result in results:
         result.start()
-    spread[...] = jnp.zeros_like(spread)
+    spread[2 * blocks] = jnp.zeros(spread.shape[1:], F32)
     add = backward_body(spread, swapped, blocks)
     tile_loop(list_ref, group_ref[0, 2], 0, hub_turns, tiles_ref, store, None, add)
     tile_loop(

time: 137 us -> 136 us (level)
  no operation moved by 1% of the time
where the time goes in v3:
time: 136 us; the launch traced here: 135 us
  Pallas kernels  52.5 us (39%)
  blocking collectives  44.6 us (33%)
  waiting for transfers between devices  21 us (15%)
  starting transfers between devices  11.9 us (9%)
  local copies, waits for them, and re-layouts  3.54 us (3%)
  between operations  1.49 us (1%)
    all_to_all x1, blocking collectives, body(): lax.all_to_all(outgoing, 'dom', split_axis=0, concat_axis=0, tiled=True)  44.6 us
    all_to_all x1, waiting for transfers between devices, body(): lax.all_to_all(grads, 'dom', split_axis=0, concat_axis=0, tiled=True)  21 us
    pallas_call x1, Pallas kernels, middle(): pl.pallas_call(middle_kernel, name='middle', in_specs=[whole(SMEM)] * 2 +...  16.8 us
    all_to_all x1, starting transfers between devices, body(): lax.all_to_all(grads, 'dom', split_axis=0, concat_axis=0, tiled=True)  11.9 us
    pallas_call x1, Pallas kernels, returned_rows(): pl.pallas_call(returned_kernel, name='returned_rows', in_specs=[whole(SME...  9.08 us
    pallas_call x1, Pallas kernels, own_backward(): pl.pallas_call(own_backward_kernel, name='own_backward', in_specs=[whole(...  7.48 us
    pallas_call x1, Pallas kernels, outgoing_rows(): pl.pallas_call(outgoing_kernel, name='outgoing_rows', in_specs=[whole(SME...  6.42 us
    pallas_call x1, Pallas kernels, boundary_forward(): pl.pallas_call(boundary_forward_kernel, name='boundary_forward', in_specs...  5 us
  transfers between devices with their start and end apart: 2, of which 1 were waited for; matrix products, arithmetic and copies ran while one was open for 0% of the time, Pallas kernels for 15%

profile of v3, /device:TPU:0, one launch (start us, length us, event | category | flops | bytes accessed | tf_op | source)
XLA Modules:
  0.0 135.0 jit_solution(2452603207193454374)
XLA Ops:
  0.6 6.4 %outgoing_rows.1 = bf16[128,72,128]{2,1,0:T(8,128)(2,1)} custom-call(s32[32,128]{1,0:T(8,128)} %bitcast.16, bf16[4096,128]{1,0:T(8,128)(2,1)} %feat_ref.1, bf16[64,128]{1,0:T(8,128)(2,1)} %hub_ref.1, s32[32,128]{1,0:T(8,128)} %bitcast.19), custom_call_target="tpu_custom_call" | custom-call | bytes 31457280 | tf_op jit(solution)/shard_map/outgoing_rows/pallas_call | solution.py:75
  7.1 0.0 copy-start.2
  7.1 44.6 %all_to_all.10.near_ref.names_ref = bf16[128,72,128]{2,1,0:T(8,128)(2,1)S(1)} all-to-all(bf16[128,72,128]{2,1,0:T(8,128)(2,1)} %outgoing_rows.1), channel_id=1, replica_groups=mesh['dom'=128] {'dom'}, dimensions={0} | all-to-all | bytes 4718592 | tf_op jit(solution)/shard_map/all_to_all | solution.py:554
  51.7 0.0 collective-permute-start
  52.3 3.6 %plan.1 = (s32[1,768]{1,0:T(1,128)}, s32[1,128]{1,0:T(1,128)}, bf16[32,128,256]{2,1,0:T(8,128)(2,1)}) custom-call(s32[1]{0:T(128)S(6)} %copy.13.count_ref, s32[1]{0:T(128)} %bitcast.side_ref, s32[2,512]{1,0:T(2,128)} %bitcast.22, s32[32,128]{1,0:T(8,128)} %bitcast.20), custom_call_target="tpu_custom_call" | custom-call | flops 10000000 | bytes 8388608 | tf_op jit(solution)/shard_map/plan/pallas_call | solution.py:156
  55.9 0.0 copy-done.2
  55.9 0.7 copy-done.8
  56.6 0.7 copy-done.11
  57.3 4.1 %own_forward.1.start_ref = f32[32,128,128]{2,1,0:T(8,128)S(1)} custom-call(s32[1,768]{1,0:T(1,128)S(1)} %copy-done.8, s32[1,128]{1,0:T(1,128)S(1)} %copy-done.11, bf16[32,128,128]{2,1,0:T(8,128)(2,1)S(1)} %bitcast.13, bf16[512,128,128]{2,1,0:T(8,128)(2,1)} %tiles_ref.7), custom_call_target="tpu_custom_call" | custom-call | flops 1000000000 | bytes 41943040 | tf_op jit(solution)/shard_map/own_forward/pallas_call | solution.py:250
  61.4 0.0 copy-start.1
  61.4 0.0 copy-start.3
  61.4 0.0 copy-start.5
  61.4 0.0 copy-start.9
  61.4 0.0 copy-start.10
  61.4 0.0 copy-start.12
  61.4 0.0 copy-start.13
  61.5 5.0 %boundary_forward.1.part_ref = f32[32,128,128]{2,1,0:T(8,128)S(1)} custom-call(s32[1,768]{1,0:T(1,128)S(1)} %copy-done.8, s32[1,128]{1,0:T(1,128)S(1)} %copy-done.11, bf16[128,72,128]{2,1,0:T(8,128)(2,1)S(1)} %all_to_all.10.near_ref.names_ref, bf16[512,128,128]{2,1,0:T(8,128)(2,1)} %tiles_ref.7), custom_call_target="tpu_custom_call" | custom-call | flops 1000000000 | bytes 41943040 | tf_op jit(solution)/shard_map/boundary_forward/pallas_call | solution.py:280
  66.5 0.0 copy-done.1
  66.5 0.0 collective-permute-done.far_ref
  66.5 0.0 copy-done
  66.5 0.0 copy-done.3
  66.5 0.0 copy-done.5
  66.5 0.0 copy-done.9
  66.5 0.0 copy-done.10
  66.6 16.8 %middle.1 = (bf16[32,128,128]{2,1,0:T(8,128)(2,1)}, bf16[32,128,128]{2,1,0:T(8,128)(2,1)}, bf16[128,64,128]{2,1,0:T(8,128)(2,1)}) custom-call(s32[1,768]{1,0:T(1,128)S(1)} %copy-done.9, s32[1,128]{1,0:T(1,128)S(1)} %copy-done.12, bf16[128,72,128]{2,1,0:T(8,128)(2,1)S(1)} %all_to_all.10.near_ref.names_ref, ...), custom_call_target="tpu_custom_call" | custom-call | flops 4000000000 | bytes 62914560 | tf_op jit(solution)/shard_map/middle/pallas_call | solution.py:379
  83.4 11.9 %all-to-all-start.1 = ((bf16[128,64,128]{2,1,0:T(8,128)(2,1)}), bf16[128,64,128]{2,1,0:T(8,128)(2,1)S(1)}, u32[]{:S(2)}, u32[]{:S(2)}) async-start(bf16[128,64,128]{2,1,0:T(8,128)(2,1)} %get-tuple-element.19), calls=%async_computation.1 | async-start | bytes 4194304 | tf_op jit(solution)/shard_map/all_to_all | solution.py:562
  95.3 0.0 copy-start.7
  95.3 7.5 %own_backward.1 = (f32[32,128,128]{2,1,0:T(8,128)S(1)}, bf16[32,64,128]{2,1,0:T(8,128)(2,1)S(1)}) custom-call(s32[1,768]{1,0:T(1,128)S(1)} %copy-done.9, s32[1,128]{1,0:T(1,128)S(1)} %copy-done.12, bf16[32,128,128]{2,1,0:T(8,128)(2,1)} %get-tuple-element.17.back_ref, bf16[128,72,128]{2,1,0:T(8,128)(2,1)} %copy-done, bf16[512,128,128]{2,1,0:T(8,128)(2,1)} %tiles_ref.7), custom_call_target="tpu_custom_call" | custom-call | flops 1000000000 | bytes 41943040 | tf_op jit(solution)/shard_map/own_backward/pallas_call | solution.py:444
  102.8 1.3 copy-done.4
  104.1 0.8 copy-done.6
  104.9 21.0 %all-to-all-done.1.back_ref = bf16[128,64,128]{2,1,0:T(8,128)(2,1)S(1)} async-done(((bf16[128,64,128]{2,1,0:T(8,128)(2,1)}), bf16[128,64,128]{2,1,0:T(8,128)(2,1)S(1)}, u32[]{:S(2)}, u32[]{:S(2)}) %all-to-all-start.1) | async-done | bytes 2097184 | tf_op jit(solution)/shard_map/all_to_all | solution.py:562
  125.9 9.1 %returned_rows.1 = (f32[4096,128]{1,0:T(8,128)}, f32[64,128]{1,0:T(8,128)}) custom-call(s32[32,128]{1,0:T(8,128)S(1)} %bitcast.17, f32[4096,128]{1,0:T(8,128)} %bitcast.14, bf16[128,64,128]{2,1,0:T(8,128)(2,1)S(1)} %all-to-all-done.1.back_ref, bf16[32,64,128]{2,1,0:T(8,128)(2,1)} %copy-done.6), custom_call_target="tpu_custom_call" | custom-call | flops 100000000 | bytes 41943040 | tf_op jit(solution)/shard_map/returned_rows/pallas_call | solution.py:519
  (8 shorter events, 0.0 us)
Async XLA Ops:
  7.1 48.9 %copy-start.2 = (bf16[4096,128]{1,0:T(8,128)(2,1)S(1)}, bf16[4096,128]{1,0:T(8,128)(2,1)}, u32[]{:S(2)}) copy-start(bf16[4096,128]{1,0:T(8,128)(2,1)} %feat_ref.1) | copy-start | bytes 3145732
  51.6 14.8 %copy-start = (bf16[128,72,128]{2,1,0:T(8,128)(2,1)}, bf16[128,72,128]{2,1,0:T(8,128)(2,1)S(1)}, u32[]{:S(2)}) copy-start(bf16[128,72,128]{2,1,0:T(8,128)(2,1)S(1)} %all_to_all.10.near_ref.names_ref) | copy-start | bytes 7077892
  51.7 14.8 %collective-permute-start = (bf16[128,72,128]{2,1,0:T(8,128)(2,1)S(1)}, bf16[128,72,128]{2,1,0:T(8,128)(2,1)}, u32[]{:S(2)}, u32[]{:S(2)}) collective-permute-start(bf16[128,72,128]{2,1,0:T(8,128)(2,1)S(1)} %all_to_all.10.near_ref.names_ref), channel_id=1, source_target_pairs={{0,1},{1,0},{2,3},{3,2},{4,5},{5,4},{6,7},{7,6},{8,9},{9,8},{10,11... | collective-permute-start | bytes 7077896 | tf_op jit(solution)/shard_map/ppermute | solution.py:557
  55.9 0.7 copy-start.8
  56.6 0.7 copy-start.11
  61.4 5.1 %copy-start.1 = (f32[32,128,128]{2,1,0:T(8,128)}, f32[32,128,128]{2,1,0:T(8,128)S(1)}, u32[]{:S(2)}) copy-start(f32[32,128,128]{2,1,0:T(8,128)S(1)} %own_forward.1.start_ref) | copy-start | bytes 6291460
  61.4 5.1 %copy-start.3 = (bf16[32,128,256]{2,1,0:T(8,128)(2,1)S(1)}, bf16[32,128,256]{2,1,0:T(8,128)(2,1)}, u32[]{:S(2)}) copy-start(bf16[32,128,256]{2,1,0:T(8,128)(2,1)} %get-tuple-element.15.hot_ref) | copy-start | bytes 6291460
  61.4 5.1 %copy-start.5 = (bf16[4096,128]{1,0:T(8,128)(2,1)S(1)}, bf16[4096,128]{1,0:T(8,128)(2,1)}, u32[]{:S(2)}) copy-start(bf16[4096,128]{1,0:T(8,128)(2,1)} %param.14) | copy-start | bytes 3145732
  61.4 5.1 %copy-start.9 = (s32[1,768]{1,0:T(1,128)S(1)}, s32[1,768]{1,0:T(1,128)}, u32[]{:S(2)}) copy-start(s32[1,768]{1,0:T(1,128)} %get-tuple-element.13.list_ref) | copy-start | bytes 9220
  61.4 5.1 %copy-start.10 = (bf16[128,128]{1,0:T(8,128)(2,1)S(1)}, bf16[128,128]{1,0:T(8,128)(2,1)}, u32[]{:S(2)}) copy-start(bf16[128,128]{1,0:T(8,128)(2,1)} %weight_ref.1) | copy-start | bytes 98308
  61.4 5.1 %copy-start.12 = (s32[1,128]{1,0:T(1,128)S(1)}, s32[1,128]{1,0:T(1,128)}, u32[]{:S(2)}) copy-start(s32[1,128]{1,0:T(1,128)} %get-tuple-element.14.group_ref) | copy-start | bytes 1540
  61.4 5.1 %copy-start.13 = (f32[128]{0:T(128)S(1)}, f32[128]{0:T(128)}, u32[]{:S(2)}) copy-start(f32[128]{0:T(128)} %param.13) | copy-start | bytes 1540
  83.4 42.5 %all-to-all-start.1 = ((bf16[128,64,128]{2,1,0:T(8,128)(2,1)}), bf16[128,64,128]{2,1,0:T(8,128)(2,1)S(1)}, u32[]{:S(2)}, u32[]{:S(2)}) async-start(bf16[128,64,128]{2,1,0:T(8,128)(2,1)} %get-tuple-element.19), calls=%async_computation.1 | async-start | bytes 4194304 | tf_op jit(solution)/shard_map/all_to_all | solution.py:562
  95.3 30.6 %copy-start.7 = (s32[1,128,32]{1,2,0:T(8,128)S(1)}, s32[1,128,32]{1,2,0:T(8,128)}, u32[]{:S(2)}) copy-start(s32[1,128,32]{1,2,0:T(8,128)} %param.18) | copy-start | bytes 49156
  102.8 1.3 copy-start.4
  104.1 0.8 copy-start.6
